TPU v7x, 32 devices: a whole 2x2x4 slice. The times are simulated.
32 devices in a mesh: rep: 8 (over z, x), exp: 4 (over y, core).
Axes of the slice: x: 2, y: 2, z: 4, core: 2. Of those that a mesh axis runs over, the one named last changes fastest.
Arguments:
- expert_ids: int32 [8, 512, 8], P('rep', 'exp'), may hold values from 0 to 15, as said below
- route_weights: bfloat16 [8, 512, 8], P('rep', 'exp'), may hold values from 0.049804688 to 0.59765625
- out_grad: bfloat16 [8, 512, 1024], P('rep', 'exp'), may hold values from -6 to 6
- saved_inputs: bfloat16 [8, 4, 32, 1024], P('rep', 'exp'), may hold values from -6 to 6
- gate_weight: bfloat16 [4, 1024, 384], P('exp', 'rep'), may hold values from -0.1875 to 0.1875
- up_weight: bfloat16 [4, 1024, 384], P('exp', 'rep'), may hold values from -0.1875 to 0.1875
- down_weight: bfloat16 [4, 1024, 384], P('exp', 'rep'), may hold values from -0.3125 to 0.3125
Outputs:
- input_grad: bfloat16 [8, 512, 1024], P('rep', 'exp')
- route_grad: bfloat16 [8, 512, 8], P('rep', 'exp')
- gate_grad: float32 [4, 1024, 384], P('exp', 'rep')
- up_grad: float32 [4, 1024, 384], P('exp', 'rep')
- down_grad: float32 [4, 1024, 384], P('exp', 'rep')
Inputs may be any that keep to these rules, and one draw needn't show every extreme that they name: `expert_ids`: each row names 8 different experts. Within each aligned block of 128 rows of one replica, an expert e with e % 4 == 0 is named at most 8 times; for every replica, some such expert is named exactly 8 times in each of its blocks.
All inputs are finite; a program needn't handle non-finite values.
Results may differ from a plain program's by a relative error of at most 0.014.
Values may be sent and summed in bfloat16 or wider, within the bound.
No kernel may reach another device: no remote copies, remote signals or barrier semaphores. Data moves between devices by JAX's collectives and lax.ppermute only.
A program may use at most 64 MiB of HBM per device.

v0:
```python
import jax
import jax.numpy as jnp
from jax import lax
from jax.sharding import PartitionSpec as P

TOPK = 8
EXP_DEV = 4


def slot_table(block_ids, slot_count, owners):
    flat_ids = block_ids.reshape(-1)
    chosen = flat_ids % EXP_DEV == 0
    owner_of = flat_ids // EXP_DEV
    capacity = slot_count // owners
    onehot = ((owner_of[:, None] == jnp.arange(owners)[None, :]) & chosen[:, None]).astype(
        jnp.int32
    )
    earlier = jnp.cumsum(onehot, axis=0) - onehot
    position = jnp.sum(earlier * onehot, axis=1)
    slot_of = jnp.where(chosen, owner_of * capacity + position, -1)
    return slot_of[None, :] == jnp.arange(slot_count)[:, None]


def first_contract(left, right):
    return lax.dot_general(
        left, right, (((0,), (0,)), ((), ())), preferred_element_type=jnp.float32
    )


def second_contract(left, right):
    return lax.dot_general(
        left, right, (((1,), (1,)), ((), ())), preferred_element_type=jnp.float32
    )


def body(expert_ids, route_weights, out_grad, saved_inputs, gate_weight, up_weight, down_weight):
    owners = lax.axis_size("exp")
    replicas = lax.axis_size("rep")
    tokens_here = out_grad.shape[1]
    features = out_grad.shape[2]
    hidden_width = gate_weight.shape[2]
    slot_count = saved_inputs.shape[2]
    capacity = slot_count // owners
    placed = slot_table(expert_ids[0], slot_count, owners)
    weights_flat = route_weights[0].reshape(-1)
    slot_scale = jnp.sum(
        jnp.where(placed, weights_flat[None, :], jnp.zeros((), weights_flat.dtype)), axis=1
    )
    token_hits = jnp.any(placed.reshape(slot_count, tokens_here, TOPK), axis=2)
    token_of = jnp.sum(jnp.where(token_hits, jnp.arange(tokens_here)[None, :], 0), axis=1)
    is_live = jnp.any(token_hits, axis=1)
    routed = jnp.where(is_live[:, None], out_grad[0][token_of], jnp.zeros((), jnp.bfloat16))
    arrived, arrived_scale = (
        lax.all_to_all(
            routed.reshape(owners, capacity, features),
            "exp",
            split_axis=0,
            concat_axis=0,
            tiled=True,
        ),
        lax.all_to_all(
            slot_scale.reshape(owners, capacity), "exp", split_axis=0, concat_axis=0, tiled=True
        ),
    )
    full_gate, full_up, full_down = (
        lax.all_gather(gate_weight[0], "rep", axis=0, tiled=True),
        lax.all_gather(up_weight[0], "rep", axis=0, tiled=True),
        lax.all_gather(down_weight[0], "rep", axis=0, tiled=True),
    )
    grad_rows = arrived.reshape(slot_count, features)
    scale_col = arrived_scale.reshape(slot_count, 1).astype(jnp.float32)
    inputs_here = saved_inputs[0, 0]
    pre_gate = jnp.dot(inputs_here, full_gate, preferred_element_type=jnp.float32)
    pre_up = jnp.dot(inputs_here, full_up, preferred_element_type=jnp.float32)
    sigmoid_gate = jax.nn.sigmoid(pre_gate)
    activated = pre_gate * sigmoid_gate
    hidden = (activated * pre_up).astype(jnp.bfloat16)
    raw_grad = jnp.dot(grad_rows, full_down, preferred_element_type=jnp.float32)
    slot_route = jnp.sum(hidden.astype(jnp.float32) * raw_grad, axis=1).astype(jnp.bfloat16)
    hidden_grad = scale_col * raw_grad
    scaled_rows = (scale_col * grad_rows.astype(jnp.float32)).astype(jnp.bfloat16)
    gate_delta = (
        hidden_grad * pre_up * sigmoid_gate * (1.0 + pre_gate * (1.0 - sigmoid_gate))
    ).astype(jnp.bfloat16)
    up_delta = (hidden_grad * activated).astype(jnp.bfloat16)
    back_rows = (
        second_contract(gate_delta, full_gate) + second_contract(up_delta, full_up)
    ).astype(jnp.bfloat16)
    returned, returned_route = (
        lax.all_to_all(
            back_rows.reshape(owners, capacity, features),
            "exp",
            split_axis=0,
            concat_axis=0,
            tiled=True,
        ),
        lax.all_to_all(
            slot_route.reshape(owners, capacity), "exp", split_axis=0, concat_axis=0, tiled=True
        ),
    )
    returned_flat = returned.reshape(slot_count, features)
    route_flat = returned_route.reshape(slot_count)
    combined = jax.ops.segment_sum(
        jnp.where(is_live[:, None], returned_flat.astype(jnp.float32), 0.0),
        token_of,
        num_segments=tokens_here,
    )
    input_grad = combined.astype(jnp.bfloat16)[None]
    route_grad = jnp.sum(
        jnp.where(placed, route_flat[:, None], jnp.zeros((), jnp.bfloat16)), axis=0
    )
    route_grad = route_grad.reshape(1, tokens_here, TOPK)
    joined_share = lax.psum_scatter(
        jnp.concatenate(
            [
                jnp.concatenate(
                    [
                        first_contract(inputs_here, gate_delta),
                        first_contract(inputs_here, up_delta),
                    ],
                    axis=1,
                ),
                first_contract(scaled_rows, hidden),
            ],
            axis=1,
        ),
        "rep",
        scatter_dimension=0,
        tiled=True,
    )
    gate_share = joined_share[:, :hidden_width]
    up_share = joined_share[:, hidden_width : 2 * hidden_width]
    down_share = joined_share[:, 2 * hidden_width :]
    gate_grad = (gate_share / replicas)[None]
    up_grad = (up_share / replicas)[None]
    down_grad = (down_share / replicas)[None]
    return (input_grad, route_grad, gate_grad, up_grad, down_grad)


def solution(mesh):
    in_specs = (
        P("rep", "exp", None),
        P("rep", "exp", None),
        P("rep", "exp", None),
        P("rep", "exp", None, None),
        P("exp", "rep", None),
        P("exp", "rep", None),
        P("exp", "rep", None),
    )
    out_specs = (
        P("rep", "exp", None),
        P("rep", "exp", None),
        P("exp", "rep", None),
        P("exp", "rep", None),
        P("exp", "rep", None),
    )
    return jax.shard_map(body, mesh=mesh, in_specs=in_specs, out_specs=out_specs, check_vma=False)
```

profile of v0, /device:TPU:0, one launch (start us, length us, event | category | flops | bytes accessed | tf_op | source)
XLA Modules:
  0.0 239.1 jit_solution(11610807980264724344)
XLA Ops:
  7.2 0.8 copy.44
  8.0 0.1 reshape_squeeze.8
  8.1 0.1 reshape_squeeze.9
  8.3 1.1 reduce-window.6
  9.5 0.2 slice_reduce_fusion
  9.7 0.2 reduce-window.9
  9.9 0.1 add_bitcast_fusion
  10.0 0.1 reduce_sum.54
  10.1 0.1 fusion.23
  10.2 0.7 fusion.18
  10.9 0.1 select_reduce_fusion
  11.0 0.1 broadcast_in_dim.101
  11.1 0.6 gather_fusion
  11.7 0.7 bitcast_select_fusion
  12.4 4.2 %all-to-all-start.1 = ((bf16[4,8,1024]{2,1,0:T(8,128)(2,1)}), bf16[4,8,1024]{2,1,0:T(8,128)(2,1)S(1)}, u32[]{:S(2)}, u32[]{:S(2)}) async-start(bf16[4,8,1024]{2,1,0:T(8,128)(2,1)} %bitcast_select_fusion), calls=%async_computation.1 | async-start | bytes 131072 | tf_op jit(solution)/shard_map/all_to_all | solution.py:54
  16.7 33.0 %all-gather.2 = bf16[1,1024,384]{2,1,0:T(8,128)(2,1)S(1)} all-gather(bf16[1,128,384]{2,1,0:T(8,128)(2,1)S(1)} %copy-done.2), channel_id=4, replica_groups=mesh['rep'=8,'exp'=4] {'rep'}, dimensions={1}, use_global_device_ids=true | all-gather | bytes 884736 | tf_op jit(solution)/shard_map/all_gather | solution.py:66
  49.7 32.4 %all-gather.1 = bf16[1,1024,384]{2,1,0:T(8,128)(2,1)S(1)} all-gather(bf16[1,128,384]{2,1,0:T(8,128)(2,1)S(1)} %copy-done.3), channel_id=3, replica_groups=mesh['rep'=8,'exp'=4] {'rep'}, dimensions={1}, use_global_device_ids=true | all-gather | bytes 884736 | tf_op jit(solution)/shard_map/all_gather | solution.py:67
  82.1 0.2 fusion.4
  82.3 0.2 fusion.7
  82.6 32.0 %all-gather = bf16[1,1024,384]{2,1,0:T(8,128)(2,1)S(1)} all-gather(bf16[1,128,384]{2,1,0:T(8,128)(2,1)S(1)} %copy-done.4), channel_id=2, replica_groups=mesh['rep'=8,'exp'=4] {'rep'}, dimensions={1}, use_global_device_ids=true | all-gather | bytes 884736 | tf_op jit(solution)/shard_map/all_gather | solution.py:68
  114.6 0.1 copy.48
  114.7 0.1 broadcast_in_dim.98
  114.8 0.3 multiply_reduce_fusion
  115.1 0.1 convert_element_type.84
  115.2 7.2 %all_to_all.26 = bf16[4,1,8]{2,1,0:T(2,128)(2,1)S(1)} all-to-all(bf16[4,1,8]{2,1,0:T(2,128)(2,1)S(1)} %convert_element_type.84), channel_id=1, replica_groups=mesh['rep'=8,'exp'=4] {'exp'}, dimensions={0} | all-to-all | bytes 128 | tf_op jit(solution)/shard_map/all_to_all | solution.py:97
  122.4 0.1 broadcast_in_dim.106
  122.5 0.1 fusion.25
  122.7 0.1 all_to_all.21
  122.7 6.1 %all_to_all.27 = bf16[4,1,8]{2,1,0:T(2,128)(2,1)S(1)} all-to-all(bf16[4,1,8]{2,1,0:T(2,128)(2,1)S(1)} %all_to_all.21), channel_id=1, replica_groups=mesh['rep'=8,'exp'=4] {'exp'}, dimensions={0} | all-to-all | bytes 128 | tf_op jit(solution)/shard_map/all_to_all | solution.py:61
  128.9 0.1 reshape.228
  128.9 0.1 multiply_convert_fusion.3
  129.0 0.4 convolution_bitcast_fusion
  129.4 0.4 convolution_bitcast_fusion.1
  129.8 0.4 fusion.26
  130.2 2.5 %pad_maximum_fusion = f32[1024,1152]{0,1:T(8,128)} fusion(f32[1024,384]{0,1:T(8,128)S(1)} %fusion.26, f32[1024,384]{0,1:T(8,128)S(1)} %convolution_bitcast_fusion, f32[1024,384]{0,1:T(8,128)S(1)} %convolution_bitcast_fusion.1), kind=kLoop, calls=%fused_computation.2 | loop fusion | flops 2359296 | bytes 9437184 | tf_op jit(solution)/shard_map/concatenate | solution.py:114
  132.8 0.3 fusion.2
  133.1 1.0 fusion.1
  134.1 3.3 %all-to-all-start.2 = ((bf16[4,8,1024]{2,1,0:T(8,128)(2,1)}), bf16[4,8,1024]{2,1,0:T(8,128)(2,1)S(1)}, u32[]{:S(2)}, u32[]{:S(2)}) async-start(bf16[4,8,1024]{2,1,0:T(8,128)(2,1)} %fusion.1), calls=%async_computation.2 | async-start | bytes 131072 | tf_op jit(solution)/shard_map/all_to_all | solution.py:90
  137.4 0.1 reshape.227
  137.5 0.7 copy.51
  138.1 3.3 %all-to-all-done.2 = bf16[4,8,1024]{2,1,0:T(8,128)(2,1)S(1)} async-done(((bf16[4,8,1024]{2,1,0:T(8,128)(2,1)}), bf16[4,8,1024]{2,1,0:T(8,128)(2,1)S(1)}, u32[]{:S(2)}, u32[]{:S(2)}) %all-to-all-start.2) | async-done | bytes 65568 | tf_op jit(solution)/shard_map/all_to_all | solution.py:90
  141.5 1.0 scatter_custom_fusion
  142.5 0.7 convert_bitcast_fusion
  143.3 85.4 %reduce-scatter.2.cloned.1.call-done = f32[128,1152]{0,1:T(8,128)} async-done(((f32[1024,1152]{0,1:T(8,128)}), f32[128,1152]{0,1:T(8,128)}) %reduce-scatter.2.cloned.1.call-update) | async-done | bytes 589840 | tf_op jit(solution)/shard_map/reduce_scatter | solution.py:113
  228.6 1.2 fusion.13
  229.8 0.8 copy.54
  230.6 0.8 copy.53
  231.4 0.8 copy.52
  (27 shorter events, 0.2 us)
Async XLA Ops:
  7.2 3.9 %copy-start = (bf16[1,128,1024]{2,1,0:T(8,128)(2,1)S(1)}, bf16[1,128,1024]{2,1,0:T(8,128)(2,1)}, u32[]{:S(2)}) copy-start(bf16[1,128,1024]{2,1,0:T(8,128)(2,1)} %param.9) | copy-start | bytes 786436
  7.2 9.5 %copy-start.2 = (bf16[1,128,384]{2,1,0:T(8,128)(2,1)S(1)}, bf16[1,128,384]{2,1,0:T(8,128)(2,1)}, u32[]{:S(2)}) copy-start(bf16[1,128,384]{2,1,0:T(8,128)(2,1)} %param.11) | copy-start | bytes 294916
  7.2 42.5 %copy-start.3 = (bf16[1,128,384]{2,1,0:T(8,128)(2,1)S(1)}, bf16[1,128,384]{2,1,0:T(8,128)(2,1)}, u32[]{:S(2)}) copy-start(bf16[1,128,384]{2,1,0:T(8,128)(2,1)} %param.12) | copy-start | bytes 294916
  8.2 73.9 %copy-start.1 = (bf16[1,1,32,1024]{3,2,1,0:T(8,128)(2,1)S(1)}, bf16[1,1,32,1024]{3,2,1,0:T(8,128)(2,1)}, u32[]{:S(2)}) copy-start(bf16[1,1,32,1024]{3,2,1,0:T(8,128)(2,1)} %param.10) | copy-start | bytes 196612
  12.4 102.4 %all-to-all-start.1 = ((bf16[4,8,1024]{2,1,0:T(8,128)(2,1)}), bf16[4,8,1024]{2,1,0:T(8,128)(2,1)S(1)}, u32[]{:S(2)}, u32[]{:S(2)}) async-start(bf16[4,8,1024]{2,1,0:T(8,128)(2,1)} %bitcast_select_fusion), calls=%async_computation.1 | async-start | bytes 131072 | tf_op jit(solution)/shard_map/all_to_all | solution.py:54
  16.7 65.9 %copy-start.4 = (bf16[1,128,384]{2,1,0:T(8,128)(2,1)S(1)}, bf16[1,128,384]{2,1,0:T(8,128)(2,1)}, u32[]{:S(2)}) copy-start(bf16[1,128,384]{2,1,0:T(8,128)(2,1)} %param.13) | copy-start | bytes 294916
  16.7 211.9 %reduce-scatter.2.cloned.1.call-start = ((), (), s32[]{:S(2)}) async-start(), calls=%async_computation.5 | async-start | bytes 5308416 | tf_op jit(solution)/shard_map/reduce_scatter | solution.py:113
  49.7 64.8 %copy-start.5 = (bf16[1,128,8]{1,2,0:T(8,128)(2,1)S(1)}, bf16[1,128,8]{1,2,0:T(8,128)(2,1)}, u32[]{:S(2)}) copy-start(bf16[1,128,8]{1,2,0:T(8,128)(2,1)} %param.8) | copy-start | bytes 6148
  134.1 7.4 %all-to-all-start.2 = ((bf16[4,8,1024]{2,1,0:T(8,128)(2,1)}), bf16[4,8,1024]{2,1,0:T(8,128)(2,1)S(1)}, u32[]{:S(2)}, u32[]{:S(2)}) async-start(bf16[4,8,1024]{2,1,0:T(8,128)(2,1)} %fusion.1), calls=%async_computation.2 | async-start | bytes 131072 | tf_op jit(solution)/shard_map/all_to_all | solution.py:90
Sparse Core Ops, SparseCore 0:
  132.9 95.7 reduce-scatter.1
where the time goes:
time: 240 us; the launch traced here: 239 us
  blocking collectives  111 us (46%)
  waiting for transfers between devices  88.7 us (37%)
  between operations  14.2 us (6%)
  other arithmetic  8.79 us (4%)
  starting transfers between devices  7.52 us (3%)
  local copies, waits for them, and re-layouts  5.86 us (2%)
  matrix products  3.3 us (1%)
    reduce_scatter x1, waiting for transfers between devices, body(): lax.psum_scatter(jnp.concatenate([jnp.concatenate([first_contract(inputs_...  85.4 us
    all_gather x1, blocking collectives, body(): lax.all_gather(gate_weight[0], 'rep', axis=0, tiled=True)  33 us
    all_gather x1, blocking collectives, body(): lax.all_gather(up_weight[0], 'rep', axis=0, tiled=True)  32.4 us
    all_gather x1, blocking collectives, body(): lax.all_gather(down_weight[0], 'rep', axis=0, tiled=True)  32 us
    all_to_all x1, blocking collectives, body(): lax.all_to_all(slot_route.reshape(owners, capacity), 'exp', split_axis=0,...  7.19 us
    all_to_all x1, blocking collectives, body(): lax.all_to_all(slot_scale.reshape(owners, capacity), 'exp', split_axis=0,...  6.08 us
  transfers between devices with their start and end apart: 3, of which 2 were waited for; matrix products, arithmetic and copies ran while one was open for 2% of the time, Pallas kernels for 0%

commit v1 on v0

--- a/solution.py
+++ b/solution.py
@@ -1,3 +1,4 @@
+import functools
 import jax
 import jax.numpy as jnp
 from jax import lax
@@ -5,6 +6,40 @@
 
 TOPK = 8
 EXP_DEV = 4
+
+
+def _guide_scales(slab_in, device_axis, where_dim):
+    passed = lax.axis_size(device_axis)
+    r_now = lax.axis_index(device_axis)
+    left_arr, aux, finding = (passed, r_now, slab_in.shape[where_dim])
+    tall = lax.dynamic_update_slice_in_dim(
+        jnp.zeros(
+            [ii * left_arr if p == where_dim else ii for p, ii in enumerate(slab_in.shape)],
+            slab_in.dtype,
+        ),
+        slab_in,
+        aux * finding,
+        axis=where_dim,
+    )
+    local_now = oldest = slab_in
+    for d in range(1, left_arr // 2 + 1):
+        local_now = lax.ppermute(
+            local_now, device_axis, list(map(lambda p: (p, (p + 1) % left_arr), range(left_arr)))
+        )
+        tall = lax.dynamic_update_slice_in_dim(
+            tall, local_now, (aux - d) % left_arr * finding, axis=where_dim
+        )
+        if 2 * d < left_arr:
+            oldest = lax.ppermute(
+                oldest, device_axis, list(map(lambda p: (p, (p - 1) % left_arr), range(left_arr)))
+            )
+            tall = lax.dynamic_update_slice_in_dim(
+                tall, oldest, (aux + d) % left_arr * finding, axis=where_dim
+            )
+    return tall
+
+
+apply_body = functools.partial(_guide_scales, device_axis="rep", where_dim=0)
 
 
 def slot_table(block_ids, slot_count, owners):
@@ -63,7 +98,7 @@
         ),
     )
     full_gate, full_up, full_down = (
-        lax.all_gather(gate_weight[0], "rep", axis=0, tiled=True),
+        apply_body(gate_weight[0]),
         lax.all_gather(up_weight[0], "rep", axis=0, tiled=True),
         lax.all_gather(down_weight[0], "rep", axis=0, tiled=True),
     )

time: 240 us -> 230 us (0.958)
  blocking collectives: 111 us -> 77.3 us
  starting transfers between devices: 7.52 us -> 22.2 us
  waiting for transfers between devices: 88.7 us -> 97.3 us
    all_gather x1 -> x0, blocking collectives: 33 us -> none  [body(): lax.all_gather(gate_weight[0], 'rep', axis=0, tiled=True)]
    ppermute x0 -> x7, starting transfers between devices: none -> 15.6 us  [the longest x3 12.5 us: _guide_scales(): lax.ppermute(oldest, device_axis, list(map(lambda p: (p, (p - 1) % left_a...]
    ppermute x0 -> x7, waiting for transfers between devices: none -> 12.6 us  [the longest x4 12.6 us: _guide_scales(): lax.ppermute(local_now, device_axis, list(map(lambda p: (p, (p + 1) % lef...]
    reduce_scatter x1, waiting for transfers between devices: 85.4 us -> 81.3 us  [body(): lax.psum_scatter(jnp.concatenate([jnp.concatenate([first_contract(inputs_...]
  transfers between devices with their start and end apart: 3 -> 10, of which waited for: 2 -> 5; matrix products, arithmetic and copies ran while one was open for 2% -> 4% of each run, Pallas kernels for 0% -> 0%
where the time goes in v1:
time: 230 us; the launch traced here: 229 us
  waiting for transfers between devices  97.3 us (42%)
  blocking collectives  77.3 us (34%)
  starting transfers between devices  22.2 us (10%)
  between operations  14.5 us (6%)
  other arithmetic  8.79 us (4%)
  local copies, waits for them, and re-layouts  6.06 us (3%)
  matrix products  3.31 us (1%)
    reduce_scatter x1, waiting for transfers between devices, body(): lax.psum_scatter(jnp.concatenate([jnp.concatenate([first_contract(inputs_...  81.3 us
    all_gather x1, blocking collectives, body(): lax.all_gather(down_weight[0], 'rep', axis=0, tiled=True)  32.6 us
    all_gather x1, blocking collectives, body(): lax.all_gather(up_weight[0], 'rep', axis=0, tiled=True)  32.3 us
    ppermute x4, waiting for transfers between devices, _guide_scales(): lax.ppermute(local_now, device_axis, list(map(lambda p: (p, (p + 1) % lef...  12.6 us
    ppermute x3, starting transfers between devices, _guide_scales(): lax.ppermute(oldest, device_axis, list(map(lambda p: (p, (p - 1) % left_a...  12.5 us
    all_to_all x1, blocking collectives, body(): lax.all_to_all(slot_route.reshape(owners, capacity), 'exp', split_axis=0,...  6.37 us
    all_to_all x1, blocking collectives, body(): lax.all_to_all(slot_scale.reshape(owners, capacity), 'exp', split_axis=0,...  6.08 us
  transfers between devices with their start and end apart: 10, of which 5 were waited for; matrix products, arithmetic and copies ran while one was open for 4% of the time, Pallas kernels for 0%

profile of v1, /device:TPU:0, one launch (start us, length us, event | category | flops | bytes accessed | tf_op | source)
XLA Modules:
  0.0 229.4 jit_solution(7685181578068588570)
XLA Ops:
  7.2 3.0 %collective-permute-start = (bf16[128,384]{1,0:T(8,128)(2,1)}, bf16[128,384]{1,0:T(8,128)(2,1)S(1)}, u32[]{:S(2)}, u32[]{:S(2)}) collective-permute-start(bf16[128,384]{1,0:T(8,128)(2,1)} %bitcast.102), channel_id=1, source_target_pairs={{0,4},{4,8},{8,12},{12,16},{16,20},{20,24},{24,28},{28,0},{1,5},{5... | collective-permute-start | bytes 294920 | tf_op jit(solution)/shard_map/ppermute | solution.py:26
  10.2 3.1 %collective-permute-start.1 = (bf16[128,384]{1,0:T(8,128)(2,1)}, bf16[128,384]{1,0:T(8,128)(2,1)S(1)}, u32[]{:S(2)}, u32[]{:S(2)}) collective-permute-start(bf16[128,384]{1,0:T(8,128)(2,1)} %bitcast.103), channel_id=1, source_target_pairs={{0,28},{4,0},{8,4},{12,8},{16,12},{20,16},{24,20},{28,24},{1,29},{... | collective-permute-start | bytes 294920 | tf_op jit(solution)/shard_map/ppermute | solution.py:33
  13.3 0.8 copy.44
  14.1 0.1 reshape_squeeze.8
  14.2 0.1 reshape_squeeze.9
  14.4 1.1 reduce-window.6
  15.5 0.2 slice_reduce_fusion
  15.7 0.2 reduce-window.9
  16.2 0.7 fusion.15
  16.9 0.1 select_reduce_fusion
  17.2 0.6 gather_fusion
  17.8 0.7 bitcast_select_fusion
  18.5 3.3 %all-to-all-start.1 = ((bf16[4,8,1024]{2,1,0:T(8,128)(2,1)}), bf16[4,8,1024]{2,1,0:T(8,128)(2,1)S(1)}, u32[]{:S(2)}, u32[]{:S(2)}) async-start(bf16[4,8,1024]{2,1,0:T(8,128)(2,1)} %bitcast_select_fusion), calls=%async_computation.1 | async-start | bytes 131072 | tf_op jit(solution)/shard_map/all_to_all | solution.py:89
  21.9 32.3 %all-gather.1 = bf16[1,1024,384]{2,1,0:T(8,128)(2,1)S(1)} all-gather(bf16[1,128,384]{2,1,0:T(8,128)(2,1)S(1)} %copy-done.2), channel_id=3, replica_groups=mesh['rep'=8,'exp'=4] {'rep'}, dimensions={1}, use_global_device_ids=true | all-gather | bytes 884736 | tf_op jit(solution)/shard_map/all_gather | solution.py:102
  54.1 32.6 %all-gather = bf16[1,1024,384]{2,1,0:T(8,128)(2,1)S(1)} all-gather(bf16[1,128,384]{2,1,0:T(8,128)(2,1)S(1)} %copy-done.3), channel_id=2, replica_groups=mesh['rep'=8,'exp'=4] {'rep'}, dimensions={1}, use_global_device_ids=true | all-gather | bytes 884736 | tf_op jit(solution)/shard_map/all_gather | solution.py:103
  86.7 0.2 fusion.4
  87.2 0.1 copy.48
  87.3 0.1 broadcast_in_dim.101
  87.5 4.7 %collective-permute-start.3 = (bf16[128,384]{1,0:T(8,128)(2,1)S(1)}, bf16[128,384]{1,0:T(8,128)(2,1)S(1)}, u32[]{:S(2)}, u32[]{:S(2)}) collective-permute-start(bf16[128,384]{1,0:T(8,128)(2,1)S(1)} %collective-permute-done.1), channel_id=1, source_target_pairs={{0,28},{4,0},{8,4},{12,8},{16,12},{20,16},{24,20},{28,24},{1,29},{... | collective-permute-start | bytes 294920 | tf_op jit(solution)/shard_map/ppermute | solution.py:33
  92.3 2.8 %collective-permute-done.2 = bf16[128,384]{1,0:T(8,128)(2,1)S(1)} collective-permute-done((bf16[128,384]{1,0:T(8,128)(2,1)S(1)}, bf16[128,384]{1,0:T(8,128)(2,1)S(1)}, u32[]{:S(2)}, u32[]{:S(2)}) %collective-permute-start.2) | collective-permute-done | bytes 98336 | tf_op jit(solution)/shard_map/ppermute | solution.py:26
  95.1 4.7 %collective-permute-start.5 = (bf16[128,384]{1,0:T(8,128)(2,1)S(1)}, bf16[128,384]{1,0:T(8,128)(2,1)S(1)}, u32[]{:S(2)}, u32[]{:S(2)}) collective-permute-start(bf16[128,384]{1,0:T(8,128)(2,1)S(1)} %collective-permute-done.3), channel_id=1, source_target_pairs={{0,28},{4,0},{8,4},{12,8},{16,12},{20,16},{24,20},{28,24},{1,29},{... | collective-permute-start | bytes 294920 | tf_op jit(solution)/shard_map/ppermute | solution.py:33
  99.9 2.5 %collective-permute-done.4 = bf16[128,384]{1,0:T(8,128)(2,1)S(1)} collective-permute-done((bf16[128,384]{1,0:T(8,128)(2,1)S(1)}, bf16[128,384]{1,0:T(8,128)(2,1)S(1)}, u32[]{:S(2)}, u32[]{:S(2)}) %collective-permute-start.4) | collective-permute-done | bytes 98336 | tf_op jit(solution)/shard_map/ppermute | solution.py:26
  102.5 7.2 %collective-permute-done.6 = bf16[128,384]{1,0:T(8,128)(2,1)S(1)} collective-permute-done((bf16[128,384]{1,0:T(8,128)(2,1)S(1)}, bf16[128,384]{1,0:T(8,128)(2,1)S(1)}, u32[]{:S(2)}, u32[]{:S(2)}) %collective-permute-start.6) | collective-permute-done | bytes 98336 | tf_op jit(solution)/shard_map/ppermute | solution.py:26
  109.8 0.2 convolution_bitcast_fusion.2
  110.0 0.3 multiply_reduce_fusion
  110.4 0.1 convert_element_type.84
  110.5 6.4 %all_to_all.26 = bf16[4,1,8]{2,1,0:T(2,128)(2,1)S(1)} all-to-all(bf16[4,1,8]{2,1,0:T(2,128)(2,1)S(1)} %convert_element_type.84), channel_id=1, replica_groups=mesh['rep'=8,'exp'=4] {'exp'}, dimensions={0} | all-to-all | bytes 128 | tf_op jit(solution)/shard_map/all_to_all | solution.py:132
  116.8 0.1 broadcast_in_dim.110
  116.9 0.1 fusion.22
  117.1 0.1 all_to_all.21
  117.2 6.1 %all_to_all.27 = bf16[4,1,8]{2,1,0:T(2,128)(2,1)S(1)} all-to-all(bf16[4,1,8]{2,1,0:T(2,128)(2,1)S(1)} %all_to_all.21), channel_id=1, replica_groups=mesh['rep'=8,'exp'=4] {'exp'}, dimensions={0} | all-to-all | bytes 128 | tf_op jit(solution)/shard_map/all_to_all | solution.py:96
  123.4 0.4 convolution_bitcast_fusion.1
  123.8 0.4 convolution_bitcast_fusion
  124.2 0.4 fusion.23
  124.6 2.5 %pad_maximum_fusion = f32[1024,1152]{0,1:T(8,128)} fusion(f32[1024,384]{0,1:T(8,128)S(1)} %fusion.23, f32[1024,384]{0,1:T(8,128)S(1)} %convolution_bitcast_fusion, f32[1024,384]{0,1:T(8,128)S(1)} %convolution_bitcast_fusion.1), kind=kLoop, calls=%fused_computation.2 | loop fusion | flops 2359296 | bytes 9437184 | tf_op jit(solution)/shard_map/concatenate | solution.py:149
  127.2 0.3 fusion.2
  127.5 1.0 fusion.1
  128.5 3.3 %all-to-all-start.2 = ((bf16[4,8,1024]{2,1,0:T(8,128)(2,1)}), bf16[4,8,1024]{2,1,0:T(8,128)(2,1)S(1)}, u32[]{:S(2)}, u32[]{:S(2)}) async-start(bf16[4,8,1024]{2,1,0:T(8,128)(2,1)} %fusion.1), calls=%async_computation.2 | async-start | bytes 131072 | tf_op jit(solution)/shard_map/all_to_all | solution.py:125
  131.8 0.1 reshape.227
  131.9 0.7 copy.51
  132.5 3.3 %all-to-all-done.2 = bf16[4,8,1024]{2,1,0:T(8,128)(2,1)S(1)} async-done(((bf16[4,8,1024]{2,1,0:T(8,128)(2,1)}), bf16[4,8,1024]{2,1,0:T(8,128)(2,1)S(1)}, u32[]{:S(2)}, u32[]{:S(2)}) %all-to-all-start.2) | async-done | bytes 65568 | tf_op jit(solution)/shard_map/all_to_all | solution.py:125
  135.9 1.0 scatter_custom_fusion
  136.9 0.7 convert_bitcast_fusion
  137.7 81.3 %reduce-scatter.2.cloned.1.call-done = f32[128,1152]{0,1:T(8,128)} async-done(((f32[1024,1152]{0,1:T(8,128)}), f32[128,1152]{0,1:T(8,128)}) %reduce-scatter.2.cloned.1.call-update) | async-done | bytes 589840 | tf_op jit(solution)/shard_map/reduce_scatter | solution.py:148
  219.0 1.2 fusion.10
  220.1 0.8 copy.54
  221.0 0.8 copy.53
  221.8 0.8 copy.52
  (49 shorter events, 1.1 us)
Async XLA Ops:
  7.2 10.0 %copy-start = (bf16[1,128,1024]{2,1,0:T(8,128)(2,1)S(1)}, bf16[1,128,1024]{2,1,0:T(8,128)(2,1)}, u32[]{:S(2)}) copy-start(bf16[1,128,1024]{2,1,0:T(8,128)(2,1)} %param.9) | copy-start | bytes 786436
  7.2 14.7 %copy-start.2 = (bf16[1,128,384]{2,1,0:T(8,128)(2,1)S(1)}, bf16[1,128,384]{2,1,0:T(8,128)(2,1)}, u32[]{:S(2)}) copy-start(bf16[1,128,384]{2,1,0:T(8,128)(2,1)} %param.12) | copy-start | bytes 294916
  7.2 46.9 %copy-start.3 = (bf16[1,128,384]{2,1,0:T(8,128)(2,1)S(1)}, bf16[1,128,384]{2,1,0:T(8,128)(2,1)}, u32[]{:S(2)}) copy-start(bf16[1,128,384]{2,1,0:T(8,128)(2,1)} %param.13) | copy-start | bytes 294916
  7.2 80.3 %collective-permute-start = (bf16[128,384]{1,0:T(8,128)(2,1)}, bf16[128,384]{1,0:T(8,128)(2,1)S(1)}, u32[]{:S(2)}, u32[]{:S(2)}) collective-permute-start(bf16[128,384]{1,0:T(8,128)(2,1)} %bitcast.102), channel_id=1, source_target_pairs={{0,4},{4,8},{8,12},{12,16},{16,20},{20,24},{24,28},{28,0},{1,5},{5... | collective-permute-start | bytes 294920 | tf_op jit(solution)/shard_map/ppermute | solution.py:26
  10.2 77.3 %collective-permute-start.1 = (bf16[128,384]{1,0:T(8,128)(2,1)}, bf16[128,384]{1,0:T(8,128)(2,1)S(1)}, u32[]{:S(2)}, u32[]{:S(2)}) collective-permute-start(bf16[128,384]{1,0:T(8,128)(2,1)} %bitcast.103), channel_id=1, source_target_pairs={{0,28},{4,0},{8,4},{12,8},{16,12},{20,16},{24,20},{28,24},{1,29},{... | collective-permute-start | bytes 294920 | tf_op jit(solution)/shard_map/ppermute | solution.py:33
  14.3 72.4 %copy-start.1 = (bf16[1,1,32,1024]{3,2,1,0:T(8,128)(2,1)S(1)}, bf16[1,1,32,1024]{3,2,1,0:T(8,128)(2,1)}, u32[]{:S(2)}) copy-start(bf16[1,1,32,1024]{3,2,1,0:T(8,128)(2,1)} %param.10) | copy-start | bytes 196612
  18.5 91.5 %all-to-all-start.1 = ((bf16[4,8,1024]{2,1,0:T(8,128)(2,1)}), bf16[4,8,1024]{2,1,0:T(8,128)(2,1)S(1)}, u32[]{:S(2)}, u32[]{:S(2)}) async-start(bf16[4,8,1024]{2,1,0:T(8,128)(2,1)} %bitcast_select_fusion), calls=%async_computation.1 | async-start | bytes 131072 | tf_op jit(solution)/shard_map/all_to_all | solution.py:89
  21.8 197.2 %reduce-scatter.2.cloned.1.call-start = ((), (), s32[]{:S(2)}) async-start(), calls=%async_computation.5 | async-start | bytes 5308416 | tf_op jit(solution)/shard_map/reduce_scatter | solution.py:148
  21.9 65.1 %copy-start.4 = (bf16[1,128,384]{2,1,0:T(8,128)(2,1)S(1)}, bf16[1,128,384]{2,1,0:T(8,128)(2,1)}, u32[]{:S(2)}) copy-start(bf16[1,128,384]{2,1,0:T(8,128)(2,1)} %param.11) | copy-start | bytes 294916
  54.1 33.1 %copy-start.5 = (bf16[1,128,8]{1,2,0:T(8,128)(2,1)S(1)}, bf16[1,128,8]{1,2,0:T(8,128)(2,1)}, u32[]{:S(2)}) copy-start(bf16[1,128,8]{1,2,0:T(8,128)(2,1)} %param.8) | copy-start | bytes 6148
  87.5 7.7 %collective-permute-start.2 = (bf16[128,384]{1,0:T(8,128)(2,1)S(1)}, bf16[128,384]{1,0:T(8,128)(2,1)S(1)}, u32[]{:S(2)}, u32[]{:S(2)}) collective-permute-start(bf16[128,384]{1,0:T(8,128)(2,1)S(1)} %collective-permute-done), channel_id=1, source_target_pairs={{0,4},{4,8},{8,12},{12,16},{16,20},{20,24},{24,28},{28,0},{1,5},{5... | collective-permute-start | bytes 294920 | tf_op jit(solution)/shard_map/ppermute | solution.py:26
  87.5 7.6 %collective-permute-start.3 = (bf16[128,384]{1,0:T(8,128)(2,1)S(1)}, bf16[128,384]{1,0:T(8,128)(2,1)S(1)}, u32[]{:S(2)}, u32[]{:S(2)}) collective-permute-start(bf16[128,384]{1,0:T(8,128)(2,1)S(1)} %collective-permute-done.1), channel_id=1, source_target_pairs={{0,28},{4,0},{8,4},{12,8},{16,12},{20,16},{24,20},{28,24},{1,29},{... | collective-permute-start | bytes 294920 | tf_op jit(solution)/shard_map/ppermute | solution.py:33
  95.1 7.3 %collective-permute-start.4 = (bf16[128,384]{1,0:T(8,128)(2,1)S(1)}, bf16[128,384]{1,0:T(8,128)(2,1)S(1)}, u32[]{:S(2)}, u32[]{:S(2)}) collective-permute-start(bf16[128,384]{1,0:T(8,128)(2,1)S(1)} %collective-permute-done.2), channel_id=1, source_target_pairs={{0,4},{4,8},{8,12},{12,16},{16,20},{20,24},{24,28},{28,0},{1,5},{5... | collective-permute-start | bytes 294920 | tf_op jit(solution)/shard_map/ppermute | solution.py:26
  95.1 7.3 %collective-permute-start.5 = (bf16[128,384]{1,0:T(8,128)(2,1)S(1)}, bf16[128,384]{1,0:T(8,128)(2,1)S(1)}, u32[]{:S(2)}, u32[]{:S(2)}) collective-permute-start(bf16[128,384]{1,0:T(8,128)(2,1)S(1)} %collective-permute-done.3), channel_id=1, source_target_pairs={{0,28},{4,0},{8,4},{12,8},{16,12},{20,16},{24,20},{28,24},{1,29},{... | collective-permute-start | bytes 294920 | tf_op jit(solution)/shard_map/ppermute | solution.py:33
  102.5 7.3 %collective-permute-start.6 = (bf16[128,384]{1,0:T(8,128)(2,1)S(1)}, bf16[128,384]{1,0:T(8,128)(2,1)S(1)}, u32[]{:S(2)}, u32[]{:S(2)}) collective-permute-start(bf16[128,384]{1,0:T(8,128)(2,1)S(1)} %collective-permute-done.4), channel_id=1, source_target_pairs={{0,4},{4,8},{8,12},{12,16},{16,20},{20,24},{24,28},{28,0},{1,5},{5... | collective-permute-start | bytes 294920 | tf_op jit(solution)/shard_map/ppermute | solution.py:26
  128.5 7.4 %all-to-all-start.2 = ((bf16[4,8,1024]{2,1,0:T(8,128)(2,1)}), bf16[4,8,1024]{2,1,0:T(8,128)(2,1)S(1)}, u32[]{:S(2)}, u32[]{:S(2)}) async-start(bf16[4,8,1024]{2,1,0:T(8,128)(2,1)} %fusion.1), calls=%async_computation.2 | async-start | bytes 131072 | tf_op jit(solution)/shard_map/all_to_all | solution.py:125
Sparse Core Ops, SparseCore 0:
  127.3 91.6 reduce-scatter.1
